TPU v7x, 32 devices: a whole 2x2x4 slice. The times are simulated.
32 devices in a mesh: dp: 4 (over z), expert: 8 (over y, x, core).
Axes of the slice: x: 2, y: 2, z: 4, core: 2. Of those that a mesh axis runs over, the one named last changes fastest.
Arguments:
- tokens: bfloat16 [4096, 2048], P(('dp', 'expert')), may hold values from -6 to 6
- grad_out: bfloat16 [4096, 2048], P(('dp', 'expert')), may hold values from -6 to 6
- combine_weights: bfloat16 [4096, 3], P(('dp', 'expert')), may hold values from 0.099609375 to 1
- expert_ids: int32 [4096, 3], P(('dp', 'expert')), may hold values from 0 to 7, as said below
- w_in: bfloat16 [8, 2048, 1536], P('expert'), may hold values from -0.125 to 0.125
- w_out: bfloat16 [8, 2048, 768], P('expert'), may hold values from -0.21875 to 0.21875
Outputs:
- d_tokens: bfloat16 [4096, 2048], P(('dp', 'expert'))
- d_combine: bfloat16 [4096, 3], P(('dp', 'expert'))
- d_w_in: float32 [8, 2048, 1536], P('expert', 'dp')
- d_w_out: float32 [8, 2048, 768], P('expert', 'dp')
Inputs may be any that keep to these rules, and one draw needn't show every extreme that they name: `expert_ids`: each row names 3 different experts; within the 128 rows of one device no expert is named more than 96 times.
All inputs are finite; a program needn't handle non-finite values.
Results may differ from a plain program's by a relative error of at most 0.01.
Values may be sent and summed in bfloat16 or wider, within the bound.
A program may use at most 128 MiB of HBM per device.

v0:
```python
import jax
import jax.numpy as jnp
from jax import lax
from jax.sharding import PartitionSpec as P


def dot_rows(lhs, rhs):
    return lax.dot_general(lhs, rhs, (((0,), (0,)), ((), ())), preferred_element_type=jnp.float32)


def scatter_sum(part):
    return lax.psum_scatter(
        part.astype(jnp.bfloat16), "dp", scatter_dimension=0, tiled=True
    ).astype(jnp.float32)


def body(tokens, grad_out, combine_weights, expert_ids, w_in, w_out):
    experts = lax.axis_size("expert")
    tok_rows, routed = expert_ids.shape
    model_width = tokens.shape[1]
    hidden_width = w_out.shape[2]
    w_in_e = w_in[0]
    w_out_e = w_out[0]

    named = expert_ids[None, :, :] == jnp.arange(experts, dtype=jnp.int32)[:, None, None]
    dense_p = jnp.sum(jnp.where(named, combine_weights[None].astype(jnp.float32), 0.0), axis=2)
    p_rows = lax.all_to_all(
        dense_p.astype(jnp.bfloat16), "expert", split_axis=0, concat_axis=0, tiled=True
    )
    p_rows = p_rows.reshape(experts * tok_rows)[:, None].astype(jnp.float32)

    x_rows = lax.all_gather(tokens, "expert", axis=0, tiled=True)
    dy_rows = lax.all_gather(grad_out, "expert", axis=0, tiled=True)

    gate_up = jnp.dot(x_rows, w_in_e, preferred_element_type=jnp.float32)
    gate_pre = gate_up[:, :hidden_width]
    up_pre = gate_up[:, hidden_width:]
    sigmoid_gate = jax.nn.sigmoid(gate_pre)
    gate_act = gate_pre * sigmoid_gate
    hidden = (gate_act * up_pre).astype(jnp.bfloat16)

    d_output = (p_rows * dy_rows.astype(jnp.float32)).astype(jnp.bfloat16)
    d_w_out = scatter_sum(dot_rows(d_output, hidden))

    dy_hidden = jnp.dot(dy_rows, w_out_e, preferred_element_type=jnp.float32)
    d_prob = jnp.sum(hidden.astype(jnp.float32) * dy_hidden, axis=1)
    d_hidden = p_rows * dy_hidden
    d_gate = d_hidden * up_pre * (sigmoid_gate * (1.0 + gate_pre * (1.0 - sigmoid_gate)))
    d_up = d_hidden * gate_act
    d_gate_up = jnp.concatenate([d_gate, d_up], axis=1).astype(jnp.bfloat16)
    d_w_in = scatter_sum(dot_rows(x_rows, d_gate_up))

    d_rows = lax.dot_general(
        d_gate_up, w_in_e, (((1,), (1,)), ((), ())), preferred_element_type=jnp.float32
    ).astype(jnp.bfloat16)
    back_rows = lax.all_to_all(
        d_rows.reshape(experts, tok_rows, model_width),
        "expert",
        split_axis=0,
        concat_axis=0,
        tiled=True,
    )
    back_prob = lax.all_to_all(
        d_prob.astype(jnp.bfloat16).reshape(experts, tok_rows),
        "expert",
        split_axis=0,
        concat_axis=0,
        tiled=True,
    )
    d_tokens = jnp.sum(back_rows.astype(jnp.float32), axis=0).astype(jnp.bfloat16)
    d_combine = jnp.sum(
        jnp.where(named, back_prob.astype(jnp.float32)[:, :, None], 0.0), axis=0
    ).astype(jnp.bfloat16)
    return (d_tokens, d_combine, d_w_in[None], d_w_out[None])


def solution(mesh):
    placed = (
        P(("dp", "expert"), None),
        P(("dp", "expert"), None),
        P(("dp", "expert"), None),
        P(("dp", "expert"), None),
        P("expert", None, None),
        P("expert", None, None),
    )
    return jax.shard_map(
        body,
        mesh=mesh,
        in_specs=placed,
        out_specs=(
            P(("dp", "expert"), None),
            P(("dp", "expert"), None),
            P("expert", "dp", None),
            P("expert", "dp", None),
        ),
        check_vma=False,
    )
```

profile of v0, /device:TPU:0, one launch (start us, length us, event | category | flops | bytes accessed | tf_op | source)
XLA Modules:
  0.0 306.9 jit_solution(8508288842911135660)
XLA Ops:
  7.2 0.7 all-gather.5.cloned.1.call-update
  8.0 0.7 all-gather.3.cloned.1.call-update
  8.7 40.6 %all-gather.5.cloned.1.call-done = bf16[1024,2048]{1,0:T(8,128)(2,1)} async-done(((bf16[128,2048]{1,0:T(8,128)(2,1)}), bf16[1024,2048]{1,0:T(8,128)(2,1)}) %all-gather.5.cloned.1.call-update) | async-done | bytes 4194320 | tf_op jit(solution)/shard_map/all_gather | solution.py:32
  49.2 11.8 %fusion.3 = f32[1024,1536]{0,1:T(8,128)} fusion(bf16[1024,2048]{1,0:T(8,128)(2,1)} %all-gather.5.cloned.1.call-done, bf16[1,2048,1536]{2,1,0:T(8,128)(2,1)} %param.10), kind=kOutput, calls=%fused_computation.5 | convolution fusion | flops 6442450944 | bytes 16777216 | tf_op jit(solution)/shard_map/dot_general | solution.py:35
  61.0 26.7 %all-gather.3.cloned.1.call-done = bf16[1024,2048]{1,0:T(8,128)(2,1)} async-done(((bf16[128,2048]{1,0:T(8,128)(2,1)}), bf16[1024,2048]{1,0:T(8,128)(2,1)}) %all-gather.3.cloned.1.call-update) | async-done | bytes 4194320 | tf_op jit(solution)/shard_map/all_gather | solution.py:33
  87.7 8.7 %multiply_reduce_fusion = (bf16[1024]{0:T(1024)(128)(2,1)S(1)}, bf16[1024,768]{0,1:T(8,128)(2,1)}, f32[1024,768]{0,1:T(8,128)}) fusion(f32[1024,1536]{0,1:T(8,128)} %fusion.3, bf16[1024,2048]{1,0:T(8,128)(2,1)} %all-gather.3.cloned.1.call-done, bf16[1,2048,768]{2,1,0:T(8,128)(2,1)S(1)} %copy-done), kind=kOutput, calls=%fused_computation.14 | convolution fusion | flops 3228302336 | bytes 18352128 | tf_op jit(solution)/shard_map/dot_general | solution.py:45
  96.5 0.6 copy.30
  97.1 3.3 %all-to-all-start.2 = ((bf16[8,1,128]{2,1,0:T(2,128)(2,1)}), bf16[8,1,128]{2,1,0:T(2,128)(2,1)S(1)}, u32[]{:S(2)}, u32[]{:S(2)}) async-start(bf16[8,1,128]{2,1,0:T(2,128)(2,1)} %copy.30), calls=%async_computation.2 | async-start | bytes 8192 | tf_op jit(solution)/shard_map/all_to_all | solution.py:63
  100.4 4.5 %all-to-all-done.2 = bf16[8,1,128]{2,1,0:T(2,128)(2,1)S(1)} async-done(((bf16[8,1,128]{2,1,0:T(2,128)(2,1)}), bf16[8,1,128]{2,1,0:T(2,128)(2,1)S(1)}, u32[]{:S(2)}, u32[]{:S(2)}) %all-to-all-start.2) | async-done | bytes 2080 | tf_op jit(solution)/shard_map/all_to_all | solution.py:63
  104.9 0.6 select_reduce_fusion
  105.5 7.0 %all_to_all.17 = bf16[8,1,128]{2,1,0:T(2,128)(2,1)S(1)} all-to-all(bf16[8,1,128]{2,1,0:T(2,128)(2,1)S(1)} %copy.27), channel_id=1, replica_groups=mesh['dp'=4,'expert'=8] {'expert'}, dimensions={0} | all-to-all | bytes 4096 | tf_op jit(solution)/shard_map/all_to_all | solution.py:27
  112.6 8.2 %fusion.10 = bf16[2048,768]{1,0:T(8,128)(2,1)} fusion(bf16[1024,768]{0,1:T(8,128)(2,1)} %get-tuple-element.23, bf16[1024,2048]{1,0:T(8,128)(2,1)} %all-gather.3.cloned.1.call-done, f32[1024]{0:T(1024)S(1)} %bitcast.34), kind=kOutput, calls=%fused_computation.10 | convolution fusion | flops 3229089792 | bytes 8916992 | tf_op jit(solution)/shard_map/dot_general | solution.py:8
  120.8 0.2 reduce-scatter.3.cloned.1.call-start
  121.0 4.8 %multiply_convert_fusion.6 = (bf16[1024,768]{0,1:T(8,128)(2,1)S(1)}, bf16[1024,768]{0,1:T(8,128)(2,1)S(1)}) fusion(f32[1024,1536]{0,1:T(8,128)} %fusion.3, f32[1024,768]{0,1:T(8,128)} %get-tuple-element.26, f32[1024]{0:T(1024)S(1)} %bitcast.35), kind=kLoop, calls=%fused_computation.17 | loop fusion | flops 11010048 | bytes 12587008 | tf_op jit(solution)/shard_map/convert.5
  125.8 1.1 copy-done.1
  126.9 0.5 copy-done.2
  127.5 9.9 %fusion = bf16[2048,1536]{0,1:T(8,128)(2,1)} fusion(bf16[1024,2048]{1,0:T(8,128)(2,1)S(1)} %copy-done.5, bf16[1024,768]{0,1:T(8,128)(2,1)S(1)} %get-tuple-element.25, bf16[1024,768]{0,1:T(8,128)(2,1)S(1)} %get-tuple-element.24), kind=kOutput, calls=%fused_computation.2 | convolution fusion | flops 6451888128 | bytes 13631488 | tf_op jit(solution)/shard_map/dot_general | solution.py:8
  137.4 9.9 %fusion.7 = bf16[1024,2048]{1,0:T(8,128)(2,1)S(1)} fusion(bf16[1,2048,1536]{2,1,0:T(8,128)(2,1)} %param.10, bf16[1024,768]{0,1:T(8,128)(2,1)} %copy-done.2, bf16[1024,768]{0,1:T(8,128)(2,1)} %copy-done.1), kind=kOutput, calls=%fused_computation.9 | convolution fusion | flops 6450839552 | bytes 13631488 | tf_op jit(solution)/shard_map/dot_general | solution.py:53
  147.3 52.3 %all_to_all.18 = bf16[8,128,2048]{2,1,0:T(8,128)(2,1)} all-to-all(bf16[8,128,2048]{2,1,0:T(8,128)(2,1)S(1)} %bitcast.33), channel_id=1, replica_groups=mesh['dp'=4,'expert'=8] {'expert'}, dimensions={0} | all-to-all | bytes 8388608 | tf_op jit(solution)/shard_map/all_to_all | solution.py:56
  199.6 4.0 %reduce_sum.40 = bf16[128,2048]{1,0:T(8,128)(2,1)} reduce(bf16[8,128,2048]{2,1,0:T(8,128)(2,1)} %all_to_all.18, bf16[]{:T(256)} %constant.5.clone.1), dimensions={0}, to_apply=%region_1.2 | reduce | flops 1835008 | bytes 4718594 | tf_op jit(solution)/shard_map/reduce_sum | solution.py:70
  203.6 2.4 bitcast_convert_fusion.1
  206.0 87.3 %reduce-scatter.3.cloned.1.call-done = bf16[512,1536]{0,1:T(8,128)(2,1)} async-done(((bf16[2048,1536]{0,1:T(8,128)(2,1)}), bf16[512,1536]{0,1:T(8,128)(2,1)}) %reduce-scatter.3.cloned.1.call-update) | async-done | bytes 1572880 | tf_op jit(solution)/shard_map/reduce_scatter | solution.py:12
  293.3 3.5 %bitcast_convert_fusion = f32[1,512,1536]{1,2,0:T(8,128)} fusion(bf16[512,1536]{0,1:T(8,128)(2,1)} %reduce-scatter.3.cloned.1.call-done), kind=kLoop, calls=%fused_computation.20 | loop fusion | flops 786432 | bytes 4718592 | tf_op jit(solution)/shard_map/broadcast_in_dim | solution.py:74
  296.8 3.5 %copy.31 = f32[1,512,1536]{2,1,0:T(8,128)} copy(f32[1,512,1536]{1,2,0:T(8,128)} %bitcast_convert_fusion) | data formatting | bytes 6291456
  (20 shorter events, 0.2 us)
Async XLA Ops:
  7.2 80.6 %copy-start = (bf16[1,2048,768]{2,1,0:T(8,128)(2,1)S(1)}, bf16[1,2048,768]{2,1,0:T(8,128)(2,1)}, u32[]{:S(2)}) copy-start(bf16[1,2048,768]{2,1,0:T(8,128)(2,1)} %param.11) | copy-start | bytes 9437188
  7.2 42.0 %all-gather.5.cloned.1.call-start = ((), (), s32[]{:S(2)}) async-start(), calls=%async_computation.6 | async-start | bytes 4718592 | tf_op jit(solution)/shard_map/all_gather | solution.py:32
  7.9 79.8 %all-gather.3.cloned.1.call-start = ((), (), s32[]{:S(2)}) async-start(), calls=%async_computation.5 | async-start | bytes 4718592 | tf_op jit(solution)/shard_map/all_gather | solution.py:33
  61.0 39.4 %copy-start.4 = (bf16[128,3]{0,1:T(4,128)(2,1)S(1)}, bf16[128,3]{0,1:T(4,128)(2,1)}, u32[]{:S(2)}) copy-start(bf16[128,3]{0,1:T(4,128)(2,1)} %param.8) | copy-start | bytes 2308
  61.0 43.9 %copy-start.3 = (s32[128,3]{0,1:T(4,128)S(1)}, s32[128,3]{0,1:T(4,128)}, u32[]{:S(2)}) copy-start(s32[128,3]{0,1:T(4,128)} %param.9) | copy-start | bytes 4612
  97.1 7.9 %all-to-all-start.2 = ((bf16[8,1,128]{2,1,0:T(2,128)(2,1)}), bf16[8,1,128]{2,1,0:T(2,128)(2,1)S(1)}, u32[]{:S(2)}, u32[]{:S(2)}) async-start(bf16[8,1,128]{2,1,0:T(2,128)(2,1)} %copy.30), calls=%async_computation.2 | async-start | bytes 8192 | tf_op jit(solution)/shard_map/all_to_all | solution.py:63
  100.4 103.2 %reduce-scatter.5.cloned.1.call-start = ((), (), s32[]{:S(2)}) async-start(), calls=%async_computation.8 | async-start | bytes 3932160 | tf_op jit(solution)/shard_map/reduce_scatter | solution.py:12
  120.8 172.5 %reduce-scatter.3.cloned.1.call-start = ((), (), s32[]{:S(2)}) async-start(), calls=%async_computation.7 | async-start | bytes 7864320 | tf_op jit(solution)/shard_map/reduce_scatter | solution.py:12
  121.0 6.5 %copy-start.5 = (bf16[1024,2048]{1,0:T(8,128)(2,1)S(1)}, bf16[1024,2048]{1,0:T(8,128)(2,1)}, u32[]{:S(2)}) copy-start(bf16[1024,2048]{1,0:T(8,128)(2,1)} %all-gather.5.cloned.1.call-done) | copy-start | bytes 12582916
  125.8 1.1 copy-start.1
  125.8 1.7 copy-start.2
Sparse Core Ops, SparseCore 0:
  9.9 39.2 all-gather.4
  51.1 36.5 all-gather.2
  120.9 59.4 reduce-scatter.4
  182.6 110.6 reduce-scatter.2
where the time goes:
time: 307 us
  waiting for transfers between devices  160 us (52%)
  blocking collectives  59.3 us (19%)
  matrix products  48.5 us (16%)
  other arithmetic  15.3 us (5%)
  between operations  13.8 us (4%)
  local copies, waits for them, and re-layouts  5.81 us (2%)
  starting transfers between devices  3.65 us (1%)
    reduce_scatter x2, waiting for transfers between devices, scatter_sum(): lax.psum_scatter(part.astype(jnp.bfloat16), 'dp', scatter_dimension=0, ti...  87.3 us
    all_to_all x1, blocking collectives, body(): lax.all_to_all(d_rows.reshape(experts, tok_rows, model_width), 'expert',...  52.3 us
    all_gather x1, waiting for transfers between devices, body(): x_rows = lax.all_gather(tokens, 'expert', axis=0, tiled=True)  40.6 us
    all_gather x1, waiting for transfers between devices, body(): dy_rows = lax.all_gather(grad_out, 'expert', axis=0, tiled=True)  26.7 us
    dot_general x2, matrix products, dot_rows(): lax.dot_general(lhs, rhs, (((0,), (0,)), ((), ())), preferred_element_typ...  18.1 us
    dot_general x1, matrix products, body(): gate_up = jnp.dot(x_rows, w_in_e, preferred_element_type=jnp.float32)  11.8 us
    dot_general x1, matrix products, body(): lax.dot_general(d_gate_up, w_in_e, (((1,), (1,)), ((), ())), preferred_el...  9.88 us
    dot_general x1, matrix products, body(): dy_hidden = jnp.dot(dy_rows, w_out_e, preferred_element_type=jnp.float32)  8.73 us
  transfers between devices with their start and end apart: 5, of which 4 were waited for; matrix products, arithmetic and copies ran while one was open for 14% of the time, Pallas kernels for 0%

commit v1 on v0

--- a/solution.py
+++ b/solution.py
@@ -1,17 +1,166 @@
 import jax
 import jax.numpy as jnp
 from jax import lax
+from jax.experimental import pallas as pl
+from jax.experimental.layout import Layout, with_layout_constraint
+from jax.experimental.pallas import tpu as pltpu
 from jax.sharding import PartitionSpec as P
+
+MESH = pl.DeviceIdType.MESH
+
+
+def flipped(index, stride):
+    return index + stride - 2 * stride * ((index // stride) % 2)
+
+
+def gather_kernel(
+    x_ref, dy_ref, p_ref, x_all, dy_all, p_all, send_sem, recv_sem, p_send, p_recv, local_sem
+):
+    devices = p_all.shape[0]
+    tok_rows = x_ref.shape[0]
+    me = lax.axis_index("expert")
+    core, side, up = flipped(me, 1), flipped(me, 2), flipped(me, 4)
+    across = flipped(side, 4)
+    alls = (x_all, dy_all)
+
+    barrier = pltpu.get_barrier_semaphore()
+    for step in range(1, devices):
+        pl.semaphore_signal(
+            barrier,
+            inc=1,
+            device_id={"expert": lax.rem(me + step, devices)},
+            device_id_type=MESH,
+        )
+    pl.semaphore_wait(barrier, devices - 1)
+
+    started = []
+
+    def block(array, owner):
+        return alls[array].at[pl.ds(pl.multiple_of(owner * tok_rows, tok_rows), tok_rows)]
+
+    def send(src, array, owner, target):
+        copy = pltpu.make_async_remote_copy(
+            src_ref=src,
+            dst_ref=block(array, owner),
+            send_sem=send_sem.at[len(started)],
+            recv_sem=recv_sem.at[array, owner],
+            device_id={"expert": target},
+            device_id_type=MESH,
+        )
+        copy.start()
+        started.append(copy)
+
+    def arrived(array, owner):
+        pltpu.make_async_remote_copy(
+            src_ref=block(array, owner),
+            dst_ref=block(array, owner),
+            send_sem=send_sem.at[0],
+            recv_sem=recv_sem.at[array, owner],
+            device_id={"expert": core},
+            device_id_type=MESH,
+        ).wait_recv()
+
+    p_copies = []
+    for step in range(1, devices):
+        copy = pltpu.make_async_remote_copy(
+            src_ref=p_ref,
+            dst_ref=p_all.at[me],
+            send_sem=p_send.at[step],
+            recv_sem=p_recv.at[me],
+            device_id={"expert": lax.rem(me + step, devices)},
+            device_id_type=MESH,
+        )
+        copy.start()
+        p_copies.append(copy)
+
+    send(x_ref, 0, me, side)
+    send(dy_ref, 1, me, up)
+    send(dy_ref, 1, me, side)
+    send(x_ref, 0, me, up)
+    send(x_ref, 0, me, core)
+    send(dy_ref, 1, me, core)
+
+    own = (
+        pltpu.make_async_copy(x_ref, block(0, me), local_sem.at[0]),
+        pltpu.make_async_copy(dy_ref, block(1, me), local_sem.at[1]),
+        pltpu.make_async_copy(p_ref, p_all.at[me], local_sem.at[2]),
+    )
+    for copy in own:
+        copy.start()
+
+    def relay(array, owner, targets):
+        arrived(array, owner)
+        for target in targets:
+            send(block(array, owner), array, owner, target)
+
+    relay(0, side, (up, core))
+    relay(1, up, (side, core))
+    relay(1, side, (core,))
+    relay(0, up, (core,))
+    relay(0, across, (core,))
+    relay(1, across, (core,))
+
+    for array in range(2):
+        for owner in (core, flipped(core, 2), flipped(core, 4), flipped(across, 1)):
+            arrived(array, owner)
+    for step in range(1, devices):
+        owner = lax.rem(me + step, devices)
+        pltpu.make_async_remote_copy(
+            src_ref=p_ref,
+            dst_ref=p_all.at[owner],
+            send_sem=p_send.at[step],
+            recv_sem=p_recv.at[owner],
+            device_id={"expert": owner},
+            device_id_type=MESH,
+        ).wait_recv()
+    for copy in started + p_copies:
+        copy.wait_send()
+    for copy in own:
+        copy.wait()
+
+
+def gather_all(tokens, grad_out, dense_p, devices):
+    if devices != 8:
+        return tuple(
+            lax.all_gather(array, "expert", axis=0, tiled=tiled)
+            for array, tiled in ((tokens, True), (grad_out, True), (dense_p, False))
+        )
+    tok_rows, model_width = tokens.shape
+    whole = jax.ShapeDtypeStruct((devices * tok_rows, model_width), tokens.dtype)
+    return pl.pallas_call(
+        gather_kernel,
+        out_shape=(
+            whole,
+            whole,
+            jax.ShapeDtypeStruct((devices,) + dense_p.shape, dense_p.dtype),
+        ),
+        in_specs=[pl.BlockSpec(memory_space=pltpu.VMEM)] * 3,
+        out_specs=(
+            pl.BlockSpec(memory_space=pl.ANY),
+            pl.BlockSpec(memory_space=pl.ANY),
+            pl.BlockSpec(memory_space=pltpu.VMEM),
+        ),
+        scratch_shapes=[
+            pltpu.SemaphoreType.DMA((14,)),
+            pltpu.SemaphoreType.DMA((2, devices)),
+            pltpu.SemaphoreType.DMA((devices,)),
+            pltpu.SemaphoreType.DMA((devices,)),
+            pltpu.SemaphoreType.DMA((3,)),
+        ],
+        compiler_params=pltpu.CompilerParams(collective_id=0, has_side_effects=True),
+    )(tokens, grad_out, dense_p)
 
 
 def dot_rows(lhs, rhs):
     return lax.dot_general(lhs, rhs, (((0,), (0,)), ((), ())), preferred_element_type=jnp.float32)
 
 
+def row_major(array):
+    return with_layout_constraint(array, Layout(major_to_minor=(0, 1)))
+
+
 def scatter_sum(part):
-    return lax.psum_scatter(
-        part.astype(jnp.bfloat16), "dp", scatter_dimension=0, tiled=True
-    ).astype(jnp.float32)
+    return lax.psum_scatter(part, "dp", scatter_dimension=0, tiled=True).astype(jnp.float32)
 
 
 def body(tokens, grad_out, combine_weights, expert_ids, w_in, w_out):
@@ -24,23 +173,22 @@
 
     named = expert_ids[None, :, :] == jnp.arange(experts, dtype=jnp.int32)[:, None, None]
     dense_p = jnp.sum(jnp.where(named, combine_weights[None].astype(jnp.float32), 0.0), axis=2)
-    p_rows = lax.all_to_all(
-        dense_p.astype(jnp.bfloat16), "expert", split_axis=0, concat_axis=0, tiled=True
-    )
-    p_rows = p_rows.reshape(experts * tok_rows)[:, None].astype(jnp.float32)
-
-    x_rows = lax.all_gather(tokens, "expert", axis=0, tiled=True)
-    dy_rows = lax.all_gather(grad_out, "expert", axis=0, tiled=True)
+    x_rows, dy_rows, p_all = gather_all(tokens, grad_out, dense_p, experts)
+    p_rows = lax.dynamic_index_in_dim(p_all, lax.axis_index("expert"), 1, keepdims=False)
+    p_rows = p_rows.reshape(experts * tok_rows)[:, None]
 
     gate_up = jnp.dot(x_rows, w_in_e, preferred_element_type=jnp.float32)
     gate_pre = gate_up[:, :hidden_width]
     up_pre = gate_up[:, hidden_width:]
     sigmoid_gate = jax.nn.sigmoid(gate_pre)
     gate_act = gate_pre * sigmoid_gate
-    hidden = (gate_act * up_pre).astype(jnp.bfloat16)
+    hidden = lax.optimization_barrier((gate_act * up_pre).astype(jnp.bfloat16))
 
     d_output = (p_rows * dy_rows.astype(jnp.float32)).astype(jnp.bfloat16)
-    d_w_out = scatter_sum(dot_rows(d_output, hidden))
+    part_out, dy_rows = lax.optimization_barrier(
+        (row_major(dot_rows(d_output, hidden).astype(jnp.bfloat16)), dy_rows)
+    )
+    d_w_out = scatter_sum(part_out)
 
     dy_hidden = jnp.dot(dy_rows, w_out_e, preferred_element_type=jnp.float32)
     d_prob = jnp.sum(hidden.astype(jnp.float32) * dy_hidden, axis=1)
@@ -48,7 +196,10 @@
     d_gate = d_hidden * up_pre * (sigmoid_gate * (1.0 + gate_pre * (1.0 - sigmoid_gate)))
     d_up = d_hidden * gate_act
     d_gate_up = jnp.concatenate([d_gate, d_up], axis=1).astype(jnp.bfloat16)
-    d_w_in = scatter_sum(dot_rows(x_rows, d_gate_up))
+    part_in, d_prob, d_gate_up = lax.optimization_barrier(
+        (row_major(dot_rows(x_rows, d_gate_up).astype(jnp.bfloat16)), d_prob, d_gate_up)
+    )
+    d_w_in = scatter_sum(part_in)
 
     d_rows = lax.dot_general(
         d_gate_up, w_in_e, (((1,), (1,)), ((), ())), preferred_element_type=jnp.float32

time: 307 us -> 262 us (0.85)
  blocking collectives: 59.3 us -> 0 us
  Pallas kernels: 0 us -> 44.5 us
  waiting for transfers between devices: 160 us -> 125 us
  starting transfers between devices: 3.65 us -> 8.27 us
    all_gather x2 -> x0, waiting for transfers between devices: 67.3 us -> none  [the longest x1 40.6 us: body(): x_rows = lax.all_gather(tokens, 'expert', axis=0, tiled=True)]
    all_to_all x2 -> x0, blocking collectives: 59.3 us -> none  [the longest x1 52.3 us: body(): lax.all_to_all(d_rows.reshape(experts, tok_rows, model_width), 'expert',...]
    all_to_all x0 -> x1, waiting for transfers between devices: none -> 48.5 us  [body(): lax.all_to_all(d_rows.reshape(experts, tok_rows, model_width), 'expert',...]
    pallas_call x0 -> x1, Pallas kernels: none -> 44.5 us  [gather_all(): pl.pallas_call(gather_kernel, out_shape=(whole, whole, jax.ShapeDtypeStru...]
    reduce_scatter x2, waiting for transfers between devices: 87.3 us -> 76.1 us  [scatter_sum(): lax.psum_scatter(part, 'dp', scatter_dimension=0, tiled=True)]
    another operation x1 -> x0, other arithmetic: 4.8 us -> none
    all_to_all x0 -> x1, starting transfers between devices: none -> 4.7 us  [body(): lax.all_to_all(d_rows.reshape(experts, tok_rows, model_width), 'expert',...]
    all_to_all x1, waiting for transfers between devices: 4.47 us -> 0.01 us  [body(): lax.all_to_all(d_prob.astype(jnp.bfloat16).reshape(experts, tok_rows), 'e...]
  transfers between devices with their start and end apart: 5 -> 4, of which waited for: 4 -> 2; matrix products, arithmetic and copies ran while one was open for 14% -> 15% of each run, Pallas kernels for 0% -> 0%
where the time goes in v1:
time: 262 us
  waiting for transfers between devices  125 us (48%)
  matrix products  48.4 us (18%)
  Pallas kernels  44.5 us (17%)
  other arithmetic  16.4 us (6%)
  between operations  14.1 us (5%)
  starting transfers between devices  8.27 us (3%)
  local copies, waits for them, and re-layouts  5.43 us (2%)
    reduce_scatter x2, waiting for transfers between devices, scatter_sum(): lax.psum_scatter(part, 'dp', scatter_dimension=0, tiled=True)  76.1 us
    all_to_all x1, waiting for transfers between devices, body(): lax.all_to_all(d_rows.reshape(experts, tok_rows, model_width), 'expert',...  48.5 us
    pallas_call x1, Pallas kernels, gather_all(): pl.pallas_call(gather_kernel, out_shape=(whole, whole, jax.ShapeDtypeStru...  44.5 us
    dot_general x2, matrix products, dot_rows(): lax.dot_general(lhs, rhs, (((0,), (0,)), ((), ())), preferred_element_typ...  17.4 us
    dot_general x1, matrix products, body(): lax.dot_general(d_gate_up, w_in_e, (((1,), (1,)), ((), ())), preferred_el...  11.2 us
    dot_general x1, matrix products, body(): gate_up = jnp.dot(x_rows, w_in_e, preferred_element_type=jnp.float32)  10 us
    dot_general x1, matrix products, body(): dy_hidden = jnp.dot(dy_rows, w_out_e, preferred_element_type=jnp.float32)  9.87 us
    broadcast_in_dim x2, other arithmetic, body(): return (d_tokens, d_combine, d_w_in[None], d_w_out[None])  5.86 us
  transfers between devices with their start and end apart: 4, of which 2 were waited for; matrix products, arithmetic and copies ran while one was open for 15% of the time, Pallas kernels for 0%

profile of v1, /device:TPU:0, one launch (start us, length us, event | category | flops | bytes accessed | tf_op | source)
XLA Modules:
  0.0 261.8 jit_solution(12852287918150672293)
XLA Ops:
  7.2 0.0 reduce-scatter.5.cloned.1.call-start
  7.2 0.8 convert_element_type.46
  8.1 1.3 select_reduce_fusion.1.p_ref
  9.4 44.5 %shard_map.93 = (bf16[1024,2048]{1,0:T(8,128)(2,1)}, bf16[1024,2048]{1,0:T(8,128)(2,1)}, f32[8,8,128]{2,1,0:T(8,128)}) custom-call(bf16[128,2048]{1,0:T(8,128)(2,1)} %x_ref.1, bf16[128,2048]{1,0:T(8,128)(2,1)} %dy_ref.1, f32[8,128]{1,0:T(8,128)} %select_reduce_fusion.1.p_ref), custom_call_target="tpu_custom_call" | custom-call | tf_op jit(solution)/shard_map/pallas_call | solution.py:130
  53.9 10.0 %fusion.2 = f32[1024,1536]{1,0:T(8,128)S(1)} fusion(bf16[1024,2048]{1,0:T(8,128)(2,1)} %get-tuple-element.12, bf16[1,2048,1536]{2,1,0:T(8,128)(2,1)} %param.10), kind=kOutput, calls=%fused_computation.4 | convolution fusion | flops 6442450944 | bytes 16777216 | tf_op jit(solution)/shard_map/dot_general | solution.py:180
  63.9 2.7 %copy-done.1 = f32[1024,1536]{1,0:T(8,128)} copy-done((f32[1024,1536]{1,0:T(8,128)}, f32[1024,1536]{1,0:T(8,128)S(1)}, u32[]{:S(2)}) %copy-start.1) | copy-done | bytes 6291480
  66.6 2.0 multiply_convert_fusion.6
  68.6 0.8 constant_dynamic-slice_fusion
  69.4 8.1 %fusion.9 = bf16[2048,768]{1,0:T(8,128)(2,1)} fusion(bf16[1024,768]{1,0:T(8,128)(2,1)} %multiply_convert_fusion.6, bf16[1024,2048]{1,0:T(8,128)(2,1)} %get-tuple-element.15, f32[1024]{0:T(1024)S(1)} %bitcast.31), kind=kOutput, calls=%fused_computation.9 | convolution fusion | flops 3229089792 | bytes 8916992 | tf_op jit(solution)/shard_map/dot_general | solution.py:155
  77.5 0.2 reduce-scatter.3.cloned.1.call-start
  77.8 9.9 %multiply_convert_fusion.5 = (bf16[1024,768]{1,0:T(8,128)(2,1)S(1)}, bf16[1024,768]{1,0:T(8,128)(2,1)S(1)}, bf16[1024]{0:T(1024)(128)(2,1)S(1)}) fusion(f32[1024,1536]{1,0:T(8,128)} %copy-done.1, f32[1024]{0:T(1024)S(1)} %bitcast.32, bf16[1024,768]{1,0:T(8,128)(2,1)} %multiply_convert_fusion.6, bf16[1024,2048]{1,0:T(8,128)(2,1)} %get-tuple-element.15, ...), kind=kOutput, calls=%fused_computation.15 | convolution fusion | flops 3234593792 | bytes 18356224 | tf_op jit(solution)/shard_map/dot_general | solution.py:193
  87.6 1.9 pad_maximum_fusion
  89.6 1.4 copy-done.3
  91.0 9.2 %convolution_convert_fusion = bf16[2048,1536]{1,0:T(8,128)(2,1)} fusion(bf16[1024,2048]{1,0:T(8,128)(2,1)S(1)} %copy-done.3, bf16[1024,768]{1,0:T(8,128)(2,1)S(1)} %get-tuple-element.21, bf16[1024,768]{1,0:T(8,128)(2,1)S(1)} %get-tuple-element.20), kind=kOutput, calls=%fused_computation.1 | convolution fusion | flops 6451888128 | bytes 13631488 | tf_op jit(solution)/shard_map/dot_general | solution.py:155
  100.2 0.6 copy.25
  100.8 3.3 %all-to-all-start.1 = ((bf16[8,1,128]{2,1,0:T(2,128)(2,1)}), bf16[8,1,128]{2,1,0:T(2,128)(2,1)S(1)}, u32[]{:S(2)}, u32[]{:S(2)}) async-start(bf16[8,1,128]{2,1,0:T(2,128)(2,1)} %copy.25), calls=%async_computation.1 | async-start | bytes 8192 | tf_op jit(solution)/shard_map/all_to_all | solution.py:214
  104.1 11.2 %fusion.6 = bf16[1024,2048]{1,0:T(8,128)(2,1)} fusion(bf16[1024,1536]{1,0:T(8,128)(2,1)} %pad_maximum_fusion, bf16[1,2048,1536]{2,1,0:T(8,128)(2,1)} %param.10), kind=kOutput, calls=%fused_computation.8 | convolution fusion | flops 6444548096 | bytes 13631488 | tf_op jit(solution)/shard_map/dot_general | solution.py:204
  115.3 4.7 %all-to-all-start = ((bf16[8,128,2048]{2,1,0:T(8,128)(2,1)}), bf16[8,128,2048]{2,1,0:T(8,128)(2,1)}, u32[]{:S(2)}, u32[]{:S(2)}) async-start(bf16[8,128,2048]{2,1,0:T(8,128)(2,1)} %bitcast.29), calls=%async_computation | async-start | bytes 8388608 | tf_op jit(solution)/shard_map/all_to_all | solution.py:207
  120.0 0.6 select_reduce_fusion
  120.6 48.5 %all-to-all-done = bf16[8,128,2048]{2,1,0:T(8,128)(2,1)} async-done(((bf16[8,128,2048]{2,1,0:T(8,128)(2,1)}), bf16[8,128,2048]{2,1,0:T(8,128)(2,1)}, u32[]{:S(2)}, u32[]{:S(2)}) %all-to-all-start) | async-done | bytes 4194336 | tf_op jit(solution)/shard_map/all_to_all | solution.py:207
  169.1 3.8 %reduce_sum.41 = bf16[128,2048]{1,0:T(8,128)(2,1)} reduce(bf16[8,128,2048]{2,1,0:T(8,128)(2,1)} %all-to-all-done, bf16[]{:T(256)} %constant.15.clone.1), dimensions={0}, to_apply=%region_2.3 | reduce | flops 1835008 | bytes 4718594 | tf_op jit(solution)/shard_map/reduce_sum | solution.py:221
  173.0 2.4 bitcast_convert_fusion.1
  175.3 76.1 %reduce-scatter.3.cloned.1.call-done = bf16[512,1536]{1,0:T(8,128)(2,1)} async-done(((bf16[2048,1536]{1,0:T(8,128)(2,1)}), bf16[512,1536]{1,0:T(8,128)(2,1)}) %reduce-scatter.3.cloned.1.call-update) | async-done | bytes 1572880 | tf_op jit(solution)/shard_map/reduce_scatter | solution.py:163
  251.5 3.5 %bitcast_convert_fusion = f32[1,512,1536]{2,1,0:T(8,128)} fusion(bf16[512,1536]{1,0:T(8,128)(2,1)} %reduce-scatter.3.cloned.1.call-done), kind=kLoop, calls=%fused_computation.19 | loop fusion | flops 786432 | bytes 4718592 | tf_op jit(solution)/shard_map/broadcast_in_dim | solution.py:225
  (11 shorter events, 0.1 us)
Async XLA Ops:
  7.2 70.6 %copy-start = (bf16[1,2048,768]{2,1,0:T(8,128)(2,1)S(1)}, bf16[1,2048,768]{2,1,0:T(8,128)(2,1)}, u32[]{:S(2)}) copy-start(bf16[1,2048,768]{2,1,0:T(8,128)(2,1)} %param.11) | copy-start | bytes 9437188
  7.2 165.8 %reduce-scatter.5.cloned.1.call-start = ((), (), s32[]{:S(2)}) async-start(), calls=%async_computation.5 | async-start | bytes 3932160 | tf_op jit(solution)/shard_map/reduce_scatter | solution.py:163
  63.9 2.7 %copy-start.1 = (f32[1024,1536]{1,0:T(8,128)}, f32[1024,1536]{1,0:T(8,128)S(1)}, u32[]{:S(2)}) copy-start(f32[1024,1536]{1,0:T(8,128)S(1)} %fusion.2) | copy-start | bytes 18874372
  77.5 173.9 %reduce-scatter.3.cloned.1.call-start = ((), (), s32[]{:S(2)}) async-start(), calls=%async_computation.4 | async-start | bytes 7864320 | tf_op jit(solution)/shard_map/reduce_scatter | solution.py:163
  87.6 3.3 %copy-start.3 = (bf16[1024,2048]{1,0:T(8,128)(2,1)S(1)}, bf16[1024,2048]{1,0:T(8,128)(2,1)}, u32[]{:S(2)}) copy-start(bf16[1024,2048]{1,0:T(8,128)(2,1)} %get-tuple-element.12) | copy-start | bytes 12582916
  100.8 14.5 %all-to-all-start.1 = ((bf16[8,1,128]{2,1,0:T(2,128)(2,1)}), bf16[8,1,128]{2,1,0:T(2,128)(2,1)S(1)}, u32[]{:S(2)}, u32[]{:S(2)}) async-start(bf16[8,1,128]{2,1,0:T(2,128)(2,1)} %copy.25), calls=%async_computation.1 | async-start | bytes 8192 | tf_op jit(solution)/shard_map/all_to_all | solution.py:214
  115.3 4.7 %copy-start.2 = (s32[128,3]{0,1:T(4,128)S(1)}, s32[128,3]{0,1:T(4,128)}, u32[]{:S(2)}) copy-start(s32[128,3]{0,1:T(4,128)} %param.9) | copy-start | bytes 4612
  115.3 53.8 %all-to-all-start = ((bf16[8,128,2048]{2,1,0:T(8,128)(2,1)}), bf16[8,128,2048]{2,1,0:T(8,128)(2,1)}, u32[]{:S(2)}, u32[]{:S(2)}) async-start(bf16[8,128,2048]{2,1,0:T(8,128)(2,1)} %bitcast.29), calls=%async_computation | async-start | bytes 8388608 | tf_op jit(solution)/shard_map/all_to_all | solution.py:207
Sparse Core Ops, SparseCore 0:
  77.6 60.7 reduce-scatter.4
  140.7 110.6 reduce-scatter.2

commit v2 on v1

--- a/solution.py
+++ b/solution.py
@@ -14,7 +14,9 @@
 
 
 def gather_kernel(
-    x_ref, dy_ref, p_ref, x_all, dy_all, p_all, send_sem, recv_sem, p_send, p_recv, local_sem
+    x_ref, dy_ref, p_ref, w_ref, x_all, dy_all, p_all, gate_all, hidden_all,
+    x_buf, w_buf, gate_buf, hidden_buf,
+    send_sem, recv_sem, half_sem, p_send, p_recv, local_sem, load_sem, out_sem,
 ):
     devices = p_all.shape[0]
     tok_rows = x_ref.shape[0]
@@ -35,27 +37,36 @@
 
     started = []
 
-    def block(array, owner):
-        return alls[array].at[pl.ds(pl.multiple_of(owner * tok_rows, tok_rows), tok_rows)]
-
-    def send(src, array, owner, target):
+    half = tok_rows // 2
+    hidden_width = hidden_all.shape[1]
+
+    def block(array, owner, part=None):
+        if part is None:
+            return alls[array].at[pl.ds(pl.multiple_of(owner * tok_rows, tok_rows), tok_rows)]
+        first = pl.multiple_of(owner * tok_rows + part * half, half)
+        return alls[array].at[pl.ds(first, half)]
+
+    def arrival_sem(array, owner, part):
+        return recv_sem.at[array, owner] if part is None else half_sem.at[array, part]
+
+    def send(src, array, owner, target, part=None):
         copy = pltpu.make_async_remote_copy(
             src_ref=src,
-            dst_ref=block(array, owner),
+            dst_ref=block(array, owner, part),
             send_sem=send_sem.at[len(started)],
-            recv_sem=recv_sem.at[array, owner],
+            recv_sem=arrival_sem(array, owner, part),
             device_id={"expert": target},
             device_id_type=MESH,
         )
         copy.start()
         started.append(copy)
 
-    def arrived(array, owner):
+    def arrived(array, owner, part=None):
         pltpu.make_async_remote_copy(
-            src_ref=block(array, owner),
-            dst_ref=block(array, owner),
+            src_ref=block(array, owner, part),
+            dst_ref=block(array, owner, part),
             send_sem=send_sem.at[0],
-            recv_sem=recv_sem.at[array, owner],
+            recv_sem=arrival_sem(array, owner, part),
             device_id={"expert": core},
             device_id_type=MESH,
         ).wait_recv()
@@ -73,12 +84,10 @@
         copy.start()
         p_copies.append(copy)
 
-    send(x_ref, 0, me, side)
-    send(dy_ref, 1, me, up)
-    send(dy_ref, 1, me, side)
-    send(x_ref, 0, me, up)
-    send(x_ref, 0, me, core)
-    send(dy_ref, 1, me, core)
+    for array, src in enumerate((x_ref, dy_ref)):
+        send(src, array, me, side)
+        send(src, array, me, up)
+        send(src, array, me, core)
 
     own = (
         pltpu.make_async_copy(x_ref, block(0, me), local_sem.at[0]),
@@ -88,21 +97,64 @@
     for copy in own:
         copy.start()
 
-    def relay(array, owner, targets):
-        arrived(array, owner)
-        for target in targets:
-            send(block(array, owner), array, owner, target)
-
-    relay(0, side, (up, core))
-    relay(1, up, (side, core))
-    relay(1, side, (core,))
-    relay(0, up, (core,))
-    relay(0, across, (core,))
-    relay(1, across, (core,))
-
-    for array in range(2):
-        for owner in (core, flipped(core, 2), flipped(core, 4), flipped(across, 1)):
-            arrived(array, owner)
+    weights = pltpu.make_async_copy(w_ref, w_buf, load_sem.at[0])
+    weights.start()
+    outs = []
+
+    def pass_on(array):
+        arrived(array, side)
+        send(block(array, side, 0), array, side, up, 0)
+        arrived(array, up)
+        send(block(array, up, 1), array, up, side, 1)
+        send(block(array, side), array, side, core)
+        send(block(array, up), array, up, core)
+
+    def pass_across(array):
+        arrived(array, across, 0)
+        arrived(array, across, 1)
+        send(block(array, across), array, across, core)
+
+    def compute(stage, owner):
+        rows = pl.ds(pl.multiple_of((owner // 2) * 2 * tok_rows, 2 * tok_rows), 2 * tok_rows)
+        load = pltpu.make_async_copy(x_all.at[rows], x_buf, load_sem.at[1])
+        load.start()
+        load.wait()
+
+        def tile(j, carry):
+            gate_cols = pl.ds(pl.multiple_of(j * 256, 256), 256)
+            up_cols = pl.ds(pl.multiple_of(hidden_width + j * 256, 256), 256)
+            a = jnp.dot(x_buf[...], w_buf[:, gate_cols], preferred_element_type=jnp.float32)
+            b = jnp.dot(x_buf[...], w_buf[:, up_cols], preferred_element_type=jnp.float32)
+            gate_buf[stage, :, gate_cols] = a
+            gate_buf[stage, :, up_cols] = b
+            hidden_buf[stage, :, gate_cols] = (a * jax.nn.sigmoid(a) * b).astype(jnp.bfloat16)
+            return carry
+
+        lax.fori_loop(0, hidden_width // 256, tile, 0)
+        for copy in (
+            pltpu.make_async_copy(gate_buf.at[stage], gate_all.at[rows], out_sem.at[stage, 0]),
+            pltpu.make_async_copy(hidden_buf.at[stage], hidden_all.at[rows], out_sem.at[stage, 1]),
+        ):
+            copy.start()
+            outs.append(copy)
+
+    own[0].wait()
+    arrived(0, core)
+    weights.wait()
+    compute(0, me)
+    pass_on(0)
+    arrived(0, flipped(side, 1))
+    compute(1, side)
+    pass_on(1)
+    arrived(0, flipped(up, 1))
+    compute(2, up)
+    pass_across(0)
+    arrived(0, flipped(across, 1))
+    compute(3, across)
+    pass_across(1)
+
+    for owner in (core, flipped(side, 1), flipped(up, 1), flipped(across, 1)):
+        arrived(1, owner)
     for step in range(1, devices):
         owner = lax.rem(me + step, devices)
         pltpu.make_async_remote_copy(
@@ -115,17 +167,28 @@
         ).wait_recv()
     for copy in started + p_copies:
         copy.wait_send()
-    for copy in own:
+    for copy in own[1:]:
         copy.wait()
-
-
-def gather_all(tokens, grad_out, dense_p, devices):
+    for copy in outs:
+        copy.wait()
+
+
+def gate_hidden(gate_up):
+    hidden_width = gate_up.shape[1] // 2
+    gate_pre = gate_up[:, :hidden_width]
+    return (gate_pre * jax.nn.sigmoid(gate_pre) * gate_up[:, hidden_width:]).astype(jnp.bfloat16)
+
+
+def gather_all(tokens, grad_out, dense_p, w_in_e, devices):
+    tok_rows, model_width = tokens.shape
+    hidden_width = w_in_e.shape[1] // 2
     if devices != 8:
-        return tuple(
+        x_rows, dy_rows, p_all = (
             lax.all_gather(array, "expert", axis=0, tiled=tiled)
             for array, tiled in ((tokens, True), (grad_out, True), (dense_p, False))
         )
-    tok_rows, model_width = tokens.shape
+        gate_up = jnp.dot(x_rows, w_in_e, preferred_element_type=jnp.float32)
+        return x_rows, dy_rows, p_all, gate_up, lax.optimization_barrier(gate_hidden(gate_up))
     whole = jax.ShapeDtypeStruct((devices * tok_rows, model_width), tokens.dtype)
     return pl.pallas_call(
         gather_kernel,
@@ -133,22 +196,35 @@
             whole,
             whole,
             jax.ShapeDtypeStruct((devices,) + dense_p.shape, dense_p.dtype),
+            jax.ShapeDtypeStruct((devices * tok_rows, 2 * hidden_width), jnp.float32),
+            jax.ShapeDtypeStruct((devices * tok_rows, hidden_width), jnp.bfloat16),
         ),
-        in_specs=[pl.BlockSpec(memory_space=pltpu.VMEM)] * 3,
+        in_specs=[pl.BlockSpec(memory_space=pltpu.VMEM)] * 3 + [pl.BlockSpec(memory_space=pl.ANY)],
         out_specs=(
             pl.BlockSpec(memory_space=pl.ANY),
             pl.BlockSpec(memory_space=pl.ANY),
             pl.BlockSpec(memory_space=pltpu.VMEM),
+            pl.BlockSpec(memory_space=pl.ANY),
+            pl.BlockSpec(memory_space=pl.ANY),
         ),
         scratch_shapes=[
-            pltpu.SemaphoreType.DMA((14,)),
+            pltpu.VMEM((2 * tok_rows, model_width), tokens.dtype),
+            pltpu.VMEM(w_in_e.shape, w_in_e.dtype),
+            pltpu.VMEM((devices // 2, 2 * tok_rows, 2 * hidden_width), jnp.float32),
+            pltpu.VMEM((devices // 2, 2 * tok_rows, hidden_width), jnp.bfloat16),
+            pltpu.SemaphoreType.DMA((16,)),
             pltpu.SemaphoreType.DMA((2, devices)),
+            pltpu.SemaphoreType.DMA((2, 2)),
             pltpu.SemaphoreType.DMA((devices,)),
             pltpu.SemaphoreType.DMA((devices,)),
             pltpu.SemaphoreType.DMA((3,)),
+            pltpu.SemaphoreType.DMA((2,)),
+            pltpu.SemaphoreType.DMA((devices // 2, 2)),
         ],
-        compiler_params=pltpu.CompilerParams(collective_id=0, has_side_effects=True),
-    )(tokens, grad_out, dense_p)
+        compiler_params=pltpu.CompilerParams(
+            collective_id=0, has_side_effects=True, vmem_limit_bytes=60 * 1024 * 1024
+        ),
+    )(tokens, grad_out, dense_p, w_in_e)
 
 
 def dot_rows(lhs, rhs):
@@ -173,16 +249,16 @@
 
     named = expert_ids[None, :, :] == jnp.arange(experts, dtype=jnp.int32)[:, None, None]
     dense_p = jnp.sum(jnp.where(named, combine_weights[None].astype(jnp.float32), 0.0), axis=2)
-    x_rows, dy_rows, p_all = gather_all(tokens, grad_out, dense_p, experts)
+    x_rows, dy_rows, p_all, gate_up, hidden = gather_all(
+        tokens, grad_out, dense_p, w_in_e, experts
+    )
     p_rows = lax.dynamic_index_in_dim(p_all, lax.axis_index("expert"), 1, keepdims=False)
     p_rows = p_rows.reshape(experts * tok_rows)[:, None]
 
-    gate_up = jnp.dot(x_rows, w_in_e, preferred_element_type=jnp.float32)
     gate_pre = gate_up[:, :hidden_width]
     up_pre = gate_up[:, hidden_width:]
     sigmoid_gate = jax.nn.sigmoid(gate_pre)
     gate_act = gate_pre * sigmoid_gate
-    hidden = lax.optimization_barrier((gate_act * up_pre).astype(jnp.bfloat16))
 
     d_output = (p_rows * dy_rows.astype(jnp.float32)).astype(jnp.bfloat16)
     part_out, dy_rows = lax.optimization_barrier(

time: 262 us -> 248 us (0.947)
  matrix products: 48.4 us -> 38.4 us
  local copies, waits for them, and re-layouts: 5.43 us -> 2.79 us
    dot_general x1 -> x0, matrix products: 10 us -> none  [body(): gate_up = jnp.dot(x_rows, w_in_e, preferred_element_type=jnp.float32)]
    unnamed x8 -> x6, local copies, waits for them, and re-layouts: 4.07 us -> 1.42 us
  transfers between devices with their start and end apart: 4 -> 4, of which waited for: 2 -> 2; matrix products, arithmetic and copies ran while one was open for 15% -> 16% of each run, Pallas kernels for 0% -> 0%
where the time goes in v2:
time: 248 us; the launch traced here: 247 us
  waiting for transfers between devices  125 us (50%)
  Pallas kernels  44.4 us (18%)
  matrix products  38.4 us (15%)
  other arithmetic  14.4 us (6%)
  between operations  14.1 us (6%)
  starting transfers between devices  8.27 us (3%)
  local copies, waits for them, and re-layouts  2.79 us (1%)
    reduce_scatter x2, waiting for transfers between devices, scatter_sum(): lax.psum_scatter(part, 'dp', scatter_dimension=0, tiled=True)  76 us
    all_to_all x1, waiting for transfers between devices, body(): lax.all_to_all(d_rows.reshape(experts, tok_rows, model_width), 'expert',...  48.5 us
    pallas_call x1, Pallas kernels, gather_all(): pl.pallas_call(gather_kernel, out_shape=(whole, whole, jax.ShapeDtypeStru...  44.4 us
    dot_general x2, matrix products, dot_rows(): lax.dot_general(lhs, rhs, (((0,), (0,)), ((), ())), preferred_element_typ...  17.4 us
    dot_general x1, matrix products, body(): lax.dot_general(d_gate_up, w_in_e, (((1,), (1,)), ((), ())), preferred_el...  11.2 us
    dot_general x1, matrix products, body(): dy_hidden = jnp.dot(dy_rows, w_out_e, preferred_element_type=jnp.float32)  9.86 us
    broadcast_in_dim x2, other arithmetic, body(): return (d_tokens, d_combine, d_w_in[None], d_w_out[None])  5.86 us
  transfers between devices with their start and end apart: 4, of which 2 were waited for; matrix products, arithmetic and copies ran while one was open for 16% of the time, Pallas kernels for 0%

profile of v2, /device:TPU:0, one launch (start us, length us, event | category | flops | bytes accessed | tf_op | source)
XLA Modules:
  0.0 247.0 jit_solution(4688330738297389820)
XLA Ops:
  7.2 0.0 copy-start
  7.2 0.0 reduce-scatter.5.cloned.1.call-start
  7.2 0.8 convert_element_type.43
  8.1 1.3 select_reduce_fusion.1.p_ref
  9.4 44.4 %shard_map.93 = (bf16[1024,2048]{1,0:T(8,128)(2,1)}, bf16[1024,2048]{1,0:T(8,128)(2,1)}, f32[8,8,128]{2,1,0:T(8,128)}, f32[1024,1536]{1,0:T(8,128)}, bf16[1024,768]{1,0:T(8,128)(2,1)}) custom-call(bf16[128,2048]{1,0:T(8,128)(2,1)} %x_ref.1, bf16[128,2048]{1,0:T(8,128)(2,1)} %dy_ref.1, f32[8,128]{1,0:T(8,128)} %select_reduce_fusion.1.p_ref, ...), custom_call_target="tpu_custom_call" | custom-call | tf_op jit(solution)/shard_map/pallas_call | solution.py:193
  53.9 0.8 constant_dynamic-slice_fusion
  54.6 8.1 %fusion.2 = bf16[2048,768]{1,0:T(8,128)(2,1)} fusion(bf16[1024,768]{1,0:T(8,128)(2,1)} %get-tuple-element.17, bf16[1024,2048]{1,0:T(8,128)(2,1)} %get-tuple-element.18, f32[1024]{0:T(1024)S(1)} %bitcast.27), kind=kOutput, calls=%fused_computation.5 | convolution fusion | flops 3229089792 | bytes 8916992 | tf_op jit(solution)/shard_map/dot_general | solution.py:231
  62.8 0.0 reduce-scatter.5.cloned.1.call-update
  62.8 0.2 reduce-scatter.3.cloned.1.call-start
  63.0 9.9 %multiply_convert_fusion.5 = (bf16[1024,768]{1,0:T(8,128)(2,1)S(1)}, bf16[1024,768]{1,0:T(8,128)(2,1)S(1)}, bf16[1024]{0:T(1024)(128)(2,1)S(1)}) fusion(f32[1024,1536]{1,0:T(8,128)} %get-tuple-element.19, f32[1024]{0:T(1024)S(1)} %bitcast.28, bf16[1024,768]{1,0:T(8,128)(2,1)} %get-tuple-element.17, bf16[1024,2048]{1,0:T(8,128)(2,1)} %get-tuple-element.18, ...), kind=kOutput, calls=%fused_computation.11 | convolution fusion | flops 3234593792 | bytes 18356224 | tf_op jit(solution)/shard_map/dot_general | solution.py:269
  72.9 1.9 pad_maximum_fusion
  74.8 1.4 copy-done.2
  76.2 9.2 %convolution_convert_fusion = bf16[2048,1536]{1,0:T(8,128)(2,1)} fusion(bf16[1024,2048]{1,0:T(8,128)(2,1)S(1)} %copy-done.2, bf16[1024,768]{1,0:T(8,128)(2,1)S(1)} %get-tuple-element.25, bf16[1024,768]{1,0:T(8,128)(2,1)S(1)} %get-tuple-element.24), kind=kOutput, calls=%fused_computation.1 | convolution fusion | flops 6451888128 | bytes 13631488 | tf_op jit(solution)/shard_map/dot_general | solution.py:231
  85.5 0.0 reduce-scatter.3.cloned.1.call-update
  85.5 0.6 copy.25
  86.1 3.3 %all-to-all-start.1 = ((bf16[8,1,128]{2,1,0:T(2,128)(2,1)}), bf16[8,1,128]{2,1,0:T(2,128)(2,1)S(1)}, u32[]{:S(2)}, u32[]{:S(2)}) async-start(bf16[8,1,128]{2,1,0:T(2,128)(2,1)} %copy.25), calls=%async_computation.1 | async-start | bytes 8192 | tf_op jit(solution)/shard_map/all_to_all | solution.py:290
  89.4 11.2 %convolution_convert_fusion.1 = bf16[1024,2048]{1,0:T(8,128)(2,1)} fusion(bf16[1024,1536]{1,0:T(8,128)(2,1)} %pad_maximum_fusion, bf16[1,2048,1536]{2,1,0:T(8,128)(2,1)} %param.10), kind=kOutput, calls=%fused_computation.4 | convolution fusion | flops 6444548096 | bytes 13631488 | tf_op jit(solution)/shard_map/dot_general | solution.py:280
  100.6 4.7 %all-to-all-start = ((bf16[8,128,2048]{2,1,0:T(8,128)(2,1)}), bf16[8,128,2048]{2,1,0:T(8,128)(2,1)}, u32[]{:S(2)}, u32[]{:S(2)}) async-start(bf16[8,128,2048]{2,1,0:T(8,128)(2,1)} %bitcast.25), calls=%async_computation | async-start | bytes 8388608 | tf_op jit(solution)/shard_map/all_to_all | solution.py:283
  105.3 0.6 select_reduce_fusion
  105.9 48.5 %all-to-all-done = bf16[8,128,2048]{2,1,0:T(8,128)(2,1)} async-done(((bf16[8,128,2048]{2,1,0:T(8,128)(2,1)}), bf16[8,128,2048]{2,1,0:T(8,128)(2,1)}, u32[]{:S(2)}, u32[]{:S(2)}) %all-to-all-start) | async-done | bytes 4194336 | tf_op jit(solution)/shard_map/all_to_all | solution.py:283
  154.4 3.8 %reduce_sum.41 = bf16[128,2048]{1,0:T(8,128)(2,1)} reduce(bf16[8,128,2048]{2,1,0:T(8,128)(2,1)} %all-to-all-done, bf16[]{:T(256)} %constant.15.clone.1), dimensions={0}, to_apply=%region_2.3 | reduce | flops 1835008 | bytes 4718594 | tf_op jit(solution)/shard_map/reduce_sum | solution.py:297
  158.2 2.4 bitcast_convert_fusion.1
  160.6 76.0 %reduce-scatter.3.cloned.1.call-done = bf16[512,1536]{1,0:T(8,128)(2,1)} async-done(((bf16[2048,1536]{1,0:T(8,128)(2,1)}), bf16[512,1536]{1,0:T(8,128)(2,1)}) %reduce-scatter.3.cloned.1.call-update) | async-done | bytes 1572880 | tf_op jit(solution)/shard_map/reduce_scatter | solution.py:239
  236.6 3.5 %bitcast_convert_fusion = f32[1,512,1536]{2,1,0:T(8,128)} fusion(bf16[512,1536]{1,0:T(8,128)(2,1)} %reduce-scatter.3.cloned.1.call-done), kind=kLoop, calls=%fused_computation.13 | loop fusion | flops 786432 | bytes 4718592 | tf_op jit(solution)/shard_map/broadcast_in_dim | solution.py:301
  (7 shorter events, 0.0 us)
Async XLA Ops:
  7.2 55.9 %copy-start = (bf16[1,2048,768]{2,1,0:T(8,128)(2,1)S(1)}, bf16[1,2048,768]{2,1,0:T(8,128)(2,1)}, u32[]{:S(2)}) copy-start(bf16[1,2048,768]{2,1,0:T(8,128)(2,1)} %param.11) | copy-start | bytes 9437188
  7.2 151.1 %reduce-scatter.5.cloned.1.call-start = ((), (), s32[]{:S(2)}) async-start(), calls=%async_computation.5 | async-start | bytes 3932160 | tf_op jit(solution)/shard_map/reduce_scatter | solution.py:239
  62.8 173.8 %reduce-scatter.3.cloned.1.call-start = ((), (), s32[]{:S(2)}) async-start(), calls=%async_computation.4 | async-start | bytes 7864320 | tf_op jit(solution)/shard_map/reduce_scatter | solution.py:239
  72.9 3.3 %copy-start.2 = (bf16[1024,2048]{1,0:T(8,128)(2,1)S(1)}, bf16[1024,2048]{1,0:T(8,128)(2,1)}, u32[]{:S(2)}) copy-start(bf16[1024,2048]{1,0:T(8,128)(2,1)} %get-tuple-element.14) | copy-start | bytes 12582916
  86.1 14.5 %all-to-all-start.1 = ((bf16[8,1,128]{2,1,0:T(2,128)(2,1)}), bf16[8,1,128]{2,1,0:T(2,128)(2,1)S(1)}, u32[]{:S(2)}, u32[]{:S(2)}) async-start(bf16[8,1,128]{2,1,0:T(2,128)(2,1)} %copy.25), calls=%async_computation.1 | async-start | bytes 8192 | tf_op jit(solution)/shard_map/all_to_all | solution.py:290
  100.6 4.7 %copy-start.1 = (s32[128,3]{0,1:T(4,128)S(1)}, s32[128,3]{0,1:T(4,128)}, u32[]{:S(2)}) copy-start(s32[128,3]{0,1:T(4,128)} %param.9) | copy-start | bytes 4612
  100.6 53.8 %all-to-all-start = ((bf16[8,128,2048]{2,1,0:T(8,128)(2,1)}), bf16[8,128,2048]{2,1,0:T(8,128)(2,1)}, u32[]{:S(2)}, u32[]{:S(2)}) async-start(bf16[8,128,2048]{2,1,0:T(8,128)(2,1)} %bitcast.25), calls=%async_computation | async-start | bytes 8388608 | tf_op jit(solution)/shard_map/all_to_all | solution.py:283
Sparse Core Ops, SparseCore 0:
  62.9 60.6 reduce-scatter.4
  125.9 110.6 reduce-scatter.2

commit v3 on v2

--- a/solution.py
+++ b/solution.py
@@ -260,9 +260,9 @@
     sigmoid_gate = jax.nn.sigmoid(gate_pre)
     gate_act = gate_pre * sigmoid_gate
 
-    d_output = (p_rows * dy_rows.astype(jnp.float32)).astype(jnp.bfloat16)
+    weighted = (p_rows * hidden.astype(jnp.float32)).astype(jnp.bfloat16)
     part_out, dy_rows = lax.optimization_barrier(
-        (row_major(dot_rows(d_output, hidden).astype(jnp.bfloat16)), dy_rows)
+        (row_major(dot_rows(dy_rows, weighted).astype(jnp.bfloat16)), dy_rows)
     )
     d_w_out = scatter_sum(part_out)
 

time: 248 us -> 247 us (level)
  no operation moved by 1% of the time
where the time goes in v3:
time: 247 us
  waiting for transfers between devices  125 us (51%)
  Pallas kernels  44.4 us (18%)
  matrix products  38.2 us (15%)
  other arithmetic  14.4 us (6%)
  between operations  14.1 us (6%)
  starting transfers between devices  8.27 us (3%)
  local copies, waits for them, and re-layouts  2.79 us (1%)
    reduce_scatter x2, waiting for transfers between devices, scatter_sum(): lax.psum_scatter(part, 'dp', scatter_dimension=0, tiled=True)  76 us
    all_to_all x1, waiting for transfers between devices, body(): lax.all_to_all(d_rows.reshape(experts, tok_rows, model_width), 'expert',...  48.5 us
    pallas_call x1, Pallas kernels, gather_all(): pl.pallas_call(gather_kernel, out_shape=(whole, whole, jax.ShapeDtypeStru...  44.4 us
    dot_general x2, matrix products, dot_rows(): lax.dot_general(lhs, rhs, (((0,), (0,)), ((), ())), preferred_element_typ...  17.2 us
    dot_general x1, matrix products, body(): lax.dot_general(d_gate_up, w_in_e, (((1,), (1,)), ((), ())), preferred_el...  11.2 us
    dot_general x1, matrix products, body(): dy_hidden = jnp.dot(dy_rows, w_out_e, preferred_element_type=jnp.float32)  9.86 us
    broadcast_in_dim x2, other arithmetic, body(): return (d_tokens, d_combine, d_w_in[None], d_w_out[None])  5.86 us
  transfers between devices with their start and end apart: 4, of which 2 were waited for; matrix products, arithmetic and copies ran while one was open for 16% of the time, Pallas kernels for 0%

profile of v3, /device:TPU:0, one launch (start us, length us, event | category | flops | bytes accessed | tf_op | source)
XLA Modules:
  0.0 246.8 jit_solution(12878432181567016316)
XLA Ops:
  7.2 0.0 copy-start
  7.2 0.0 reduce-scatter.5.cloned.1.call-start
  7.2 0.8 convert_element_type.41
  8.1 1.3 select_reduce_fusion.1.p_ref
  9.4 44.4 %shard_map.93 = (bf16[1024,2048]{1,0:T(8,128)(2,1)}, bf16[1024,2048]{1,0:T(8,128)(2,1)}, f32[8,8,128]{2,1,0:T(8,128)}, f32[1024,1536]{1,0:T(8,128)}, bf16[1024,768]{1,0:T(8,128)(2,1)}) custom-call(bf16[128,2048]{1,0:T(8,128)(2,1)} %x_ref.1, bf16[128,2048]{1,0:T(8,128)(2,1)} %dy_ref.1, f32[8,128]{1,0:T(8,128)} %select_reduce_fusion.1.p_ref, ...), custom_call_target="tpu_custom_call" | custom-call | tf_op jit(solution)/shard_map/pallas_call | solution.py:193
  53.9 0.8 constant_dynamic-slice_fusion
  54.6 8.0 %convolution_convert_fusion.2 = bf16[2048,768]{1,0:T(8,128)(2,1)} fusion(bf16[1024,2048]{1,0:T(8,128)(2,1)} %get-tuple-element.18, bf16[1024,768]{1,0:T(8,128)(2,1)} %get-tuple-element.17, f32[1024]{0:T(1024)S(1)} %bitcast.27), kind=kOutput, calls=%fused_computation.4 | convolution fusion | flops 3225157632 | bytes 8916992 | tf_op jit(solution)/shard_map/dot_general | solution.py:231
  62.6 0.0 reduce-scatter.5.cloned.1.call-update
  62.6 0.2 reduce-scatter.3.cloned.1.call-start
  62.9 9.9 %multiply_convert_fusion.1 = (bf16[1024,768]{1,0:T(8,128)(2,1)S(1)}, bf16[1024,768]{1,0:T(8,128)(2,1)S(1)}, bf16[1024]{0:T(1024)(128)(2,1)S(1)}) fusion(f32[1024,1536]{1,0:T(8,128)} %get-tuple-element.19, f32[1024]{0:T(1024)S(1)} %bitcast.28, bf16[1024,768]{1,0:T(8,128)(2,1)} %get-tuple-element.17, bf16[1024,2048]{1,0:T(8,128)(2,1)} %get-tuple-element.18, ...), kind=kOutput, calls=%fused_computation.11 | convolution fusion | flops 3234593792 | bytes 18356224 | tf_op jit(solution)/shard_map/dot_general | solution.py:269
  72.7 1.9 pad_maximum_fusion
  74.6 1.4 copy-done.2
  76.1 9.2 %convolution_convert_fusion = bf16[2048,1536]{1,0:T(8,128)(2,1)} fusion(bf16[1024,2048]{1,0:T(8,128)(2,1)S(1)} %copy-done.2, bf16[1024,768]{1,0:T(8,128)(2,1)S(1)} %get-tuple-element.25, bf16[1024,768]{1,0:T(8,128)(2,1)S(1)} %get-tuple-element.24), kind=kOutput, calls=%fused_computation | convolution fusion | flops 6451888128 | bytes 13631488 | tf_op jit(solution)/shard_map/dot_general | solution.py:231
  85.3 0.0 reduce-scatter.3.cloned.1.call-update
  85.3 0.6 copy.25
  85.9 3.3 %all-to-all-start.1 = ((bf16[8,1,128]{2,1,0:T(2,128)(2,1)}), bf16[8,1,128]{2,1,0:T(2,128)(2,1)S(1)}, u32[]{:S(2)}, u32[]{:S(2)}) async-start(bf16[8,1,128]{2,1,0:T(2,128)(2,1)} %copy.25), calls=%async_computation.1 | async-start | bytes 8192 | tf_op jit(solution)/shard_map/all_to_all | solution.py:290
  89.2 11.2 %convolution_convert_fusion.1 = bf16[1024,2048]{1,0:T(8,128)(2,1)} fusion(bf16[1024,1536]{1,0:T(8,128)(2,1)} %pad_maximum_fusion, bf16[1,2048,1536]{2,1,0:T(8,128)(2,1)} %param.10), kind=kOutput, calls=%fused_computation.3 | convolution fusion | flops 6444548096 | bytes 13631488 | tf_op jit(solution)/shard_map/dot_general | solution.py:280
  100.4 4.7 %all-to-all-start = ((bf16[8,128,2048]{2,1,0:T(8,128)(2,1)}), bf16[8,128,2048]{2,1,0:T(8,128)(2,1)}, u32[]{:S(2)}, u32[]{:S(2)}) async-start(bf16[8,128,2048]{2,1,0:T(8,128)(2,1)} %bitcast.25), calls=%async_computation | async-start | bytes 8388608 | tf_op jit(solution)/shard_map/all_to_all | solution.py:283
  105.1 0.6 select_reduce_fusion
  105.7 48.5 %all-to-all-done = bf16[8,128,2048]{2,1,0:T(8,128)(2,1)} async-done(((bf16[8,128,2048]{2,1,0:T(8,128)(2,1)}), bf16[8,128,2048]{2,1,0:T(8,128)(2,1)}, u32[]{:S(2)}, u32[]{:S(2)}) %all-to-all-start) | async-done | bytes 4194336 | tf_op jit(solution)/shard_map/all_to_all | solution.py:283
  154.2 3.8 %reduce_sum.41 = bf16[128,2048]{1,0:T(8,128)(2,1)} reduce(bf16[8,128,2048]{2,1,0:T(8,128)(2,1)} %all-to-all-done, bf16[]{:T(256)} %constant.15.clone.1), dimensions={0}, to_apply=%region_2.3 | reduce | flops 1835008 | bytes 4718594 | tf_op jit(solution)/shard_map/reduce_sum | solution.py:297
  158.1 2.4 bitcast_convert_fusion.1
  160.4 76.0 %reduce-scatter.3.cloned.1.call-done = bf16[512,1536]{1,0:T(8,128)(2,1)} async-done(((bf16[2048,1536]{1,0:T(8,128)(2,1)}), bf16[512,1536]{1,0:T(8,128)(2,1)}) %reduce-scatter.3.cloned.1.call-update) | async-done | bytes 1572880 | tf_op jit(solution)/shard_map/reduce_scatter | solution.py:239
  236.4 3.5 %bitcast_convert_fusion = f32[1,512,1536]{2,1,0:T(8,128)} fusion(bf16[512,1536]{1,0:T(8,128)(2,1)} %reduce-scatter.3.cloned.1.call-done), kind=kLoop, calls=%fused_computation.13 | loop fusion | flops 786432 | bytes 4718592 | tf_op jit(solution)/shard_map/broadcast_in_dim | solution.py:301
  (7 shorter events, 0.0 us)
Async XLA Ops:
  7.2 55.7 %copy-start = (bf16[1,2048,768]{2,1,0:T(8,128)(2,1)S(1)}, bf16[1,2048,768]{2,1,0:T(8,128)(2,1)}, u32[]{:S(2)}) copy-start(bf16[1,2048,768]{2,1,0:T(8,128)(2,1)} %param.11) | copy-start | bytes 9437188
  7.2 150.9 %reduce-scatter.5.cloned.1.call-start = ((), (), s32[]{:S(2)}) async-start(), calls=%async_computation.5 | async-start | bytes 3932160 | tf_op jit(solution)/shard_map/reduce_scatter | solution.py:239
  62.6 173.8 %reduce-scatter.3.cloned.1.call-start = ((), (), s32[]{:S(2)}) async-start(), calls=%async_computation.4 | async-start | bytes 7864320 | tf_op jit(solution)/shard_map/reduce_scatter | solution.py:239
  72.7 3.3 %copy-start.2 = (bf16[1024,2048]{1,0:T(8,128)(2,1)S(1)}, bf16[1024,2048]{1,0:T(8,128)(2,1)}, u32[]{:S(2)}) copy-start(bf16[1024,2048]{1,0:T(8,128)(2,1)} %get-tuple-element.14) | copy-start | bytes 12582916
  85.9 14.5 %all-to-all-start.1 = ((bf16[8,1,128]{2,1,0:T(2,128)(2,1)}), bf16[8,1,128]{2,1,0:T(2,128)(2,1)S(1)}, u32[]{:S(2)}, u32[]{:S(2)}) async-start(bf16[8,1,128]{2,1,0:T(2,128)(2,1)} %copy.25), calls=%async_computation.1 | async-start | bytes 8192 | tf_op jit(solution)/shard_map/all_to_all | solution.py:290
  100.4 4.7 %copy-start.1 = (s32[128,3]{0,1:T(4,128)S(1)}, s32[128,3]{0,1:T(4,128)}, u32[]{:S(2)}) copy-start(s32[128,3]{0,1:T(4,128)} %param.9) | copy-start | bytes 4612
  100.4 53.8 %all-to-all-start = ((bf16[8,128,2048]{2,1,0:T(8,128)(2,1)}), bf16[8,128,2048]{2,1,0:T(8,128)(2,1)}, u32[]{:S(2)}, u32[]{:S(2)}) async-start(bf16[8,128,2048]{2,1,0:T(8,128)(2,1)} %bitcast.25), calls=%async_computation | async-start | bytes 8388608 | tf_op jit(solution)/shard_map/all_to_all | solution.py:283
Sparse Core Ops, SparseCore 0:
  62.7 60.6 reduce-scatter.4
  125.7 110.6 reduce-scatter.2
